TPU v7x, 256 devices: a whole 4x4x8 slice. The times are simulated.
256 devices in a mesh: ind: 64 (over z_hi, y, x, core), snp: 4 (over z_lo).
Axes of the slice: x: 4, y: 4, z: 8 (z_hi: 2, z_lo: 4; z = z_hi * 4 + z_lo), core: 2. Of those that a mesh axis runs over, the one named last changes fastest.
Arguments:
- dosages: bfloat16 [11264, 131072], P('ind', 'snp'), may hold values from 0 to 2, as said below
- phenotype: int32 [11264], P('ind'), may hold values 0 or 1
- mean_effect: float32 [131072], P(('snp', 'ind')), may hold values from -3 to 3
- factor: float32 [131072, 256], P(('snp', 'ind')), may hold values from -1 to 1
- log_scale: float32 [131072], P(('snp', 'ind')), may hold values from -1 to 0
- diag_noise: float32 [131072, 128], P(('snp', 'ind')), may hold values from -5 to 5
- base_points: float32 [128, 256], replicated, may hold values from -5 to 5
Outputs:
- grad_mean: float32 [131072], P(('snp', 'ind'))
- grad_factor: float32 [131072, 256], P(('snp', 'ind'))
- grad_log_scale: float32 [131072], P(('snp', 'ind'))
- mean_loglik: float32 [], replicated
- rank_entropy: float32 [], replicated
Inputs may be any that keep to these rules, and one draw needn't show every extreme that they name: `dosages`: each entry is an allele count.
All inputs are finite; a program needn't handle non-finite values. No bound on the sum of `phenotype` on one device may be relied on, other than what follows from the above.
Results may differ from a plain program's by a relative error of at most 0.00085.
The roundings to bfloat16 on the way count: a program that leaves them out, or rounds other values in their place, can miss the bound.
Values may be sent and summed in bfloat16 or wider, within the bound.
No kernel may reach another device: no remote copies, remote signals or barrier semaphores. Data moves between devices by JAX's collectives and lax.ppermute only.
A program may use at most 128 MiB of HBM per device.

v0:
```python
import math
import jax
import jax.numpy as jnp
from jax import lax
from jax.sharding import PartitionSpec as P

P_SIZE = 131072
R = 256
S = 128
COHORT_RATIO = 40


def invert_gram(gram_matrix):
    factor_chol = jnp.linalg.cholesky(gram_matrix)
    identity = jnp.eye(gram_matrix.shape[0], dtype=gram_matrix.dtype)
    lower_inv = lax.linalg.triangular_solve(factor_chol, identity, left_side=True, lower=True)
    inverse = jnp.dot(lower_inv.T, lower_inv, precision=lax.Precision.HIGHEST)
    return (factor_chol, inverse)


def on_device(dosages, phenotype, mean_effect, factor, log_scale, diag_noise, base_points):
    sample_count = base_points.shape[0]
    local_ind = dosages.shape[0]
    total_ind = local_ind * lax.axis_size("ind")
    root_p = math.sqrt(P_SIZE)
    spread = jnp.exp(log_scale)
    low_rank = jnp.dot(factor, base_points.T, precision=lax.Precision.HIGHEST)
    samples = ((mean_effect[:, None] + low_rank + spread[:, None] * diag_noise) / root_p).astype(
        jnp.bfloat16
    )
    columns = dosages
    partial_logits = jnp.dot(
        columns,
        lax.all_gather(samples, "ind", axis=0, tiled=True),
        preferred_element_type=jnp.float32,
    )
    labels = phenotype.astype(jnp.float32)[:, None]
    logits = lax.psum(partial_logits.astype(jnp.bfloat16), "snp").astype(jnp.float32)
    loglik_terms = jnp.sum(labels * logits - jax.nn.softplus(logits))
    loglik_total = lax.psum(loglik_terms, "ind")
    weights = (COHORT_RATIO * (labels - jax.nn.sigmoid(logits)) / S).astype(jnp.bfloat16)
    mean_loglik = loglik_total / (total_ind * sample_count)
    columns = dosages
    gradient = lax.psum_scatter(
        lax.dot_general(
            columns, weights, (((0,), (0,)), ((), ())), preferred_element_type=jnp.float32
        ),
        "ind",
        scatter_dimension=0,
        tiled=True,
    )
    scaled = factor / spread[:, None]
    identity = jnp.eye(R, dtype=jnp.float32)
    gram_part = jnp.dot(scaled.T, scaled, precision=lax.Precision.HIGHEST)
    gram_matrix = identity + lax.psum(gram_part, ("ind", "snp"))
    factor_chol, inverse = invert_gram(gram_matrix)
    rank_entropy = jnp.sum(jnp.log(jnp.diagonal(factor_chol))) / R
    projected = jnp.dot(factor, inverse, precision=lax.Precision.HIGHEST)
    spread_sq = spread * spread
    grad_mean = jnp.sum(gradient, axis=1) / root_p - mean_effect
    grad_factor = (
        jnp.dot(gradient, base_points, precision=lax.Precision.HIGHEST) / root_p
        - factor
        + projected / spread_sq[:, None]
    )
    leverage = jnp.sum(projected * factor, axis=1)
    grad_log_scale = (
        spread * jnp.sum(gradient * diag_noise, axis=1) / root_p
        + 1.0
        - spread_sq
        - leverage / spread_sq
    )
    return (grad_mean, grad_factor, grad_log_scale, mean_loglik, rank_entropy)


def solution(mesh):
    in_specs = (
        P("ind", "snp"),
        P("ind"),
        P(("snp", "ind")),
        P(("snp", "ind"), None),
        P(("snp", "ind")),
        P(("snp", "ind"), None),
        P(),
    )
    out_specs = (P(("snp", "ind")), P(("snp", "ind"), None), P(("snp", "ind")), P(), P())
    return jax.shard_map(
        on_device, mesh=mesh, in_specs=in_specs, out_specs=out_specs, check_vma=False
    )
```

profile of v0, /device:TPU:32, one launch (start us, length us, event | category | flops | bytes accessed | tf_op | source)
XLA Modules:
  0.0 618.1 jit_solution(5039435738711736244)
XLA Ops:
  8.1 0.7 exp.10
  8.9 2.4 fusion.4
  11.3 3.1 fusion.6
  14.5 0.7 convert_element_type.24
  15.2 112.5 %all-gather.2.cloned.1.call-done = bf16[32768,128]{1,0:T(8,128)(2,1)} async-done(((bf16[512,128]{1,0:T(8,128)(2,1)}), bf16[32768,128]{1,0:T(8,128)(2,1)}) %all-gather.2.cloned.1.call-update) | async-done | bytes 8388624 | tf_op jit(solution)/shard_map/all_gather | solution.py:34
  127.6 9.9 %fusion.5 = bf16[176,128]{1,0:T(8,128)(2,1)S(1)} fusion(bf16[176,32768]{1,0:T(8,128)(2,1)} %param.7, bf16[32768,128]{1,0:T(8,128)(2,1)} %all-gather.2.cloned.1.call-done), kind=kOutput, calls=%fused_computation.15 | convolution fusion | flops 1476417536 | bytes 19968000 | tf_op jit(solution)/shard_map/dot_general | solution.py:32
  137.5 15.6 %psum.21 = bf16[176,128]{1,0:T(8,128)(2,1)S(1)} all-reduce(bf16[176,128]{1,0:T(8,128)(2,1)S(1)} %fusion.5), channel_id=1, replica_groups=mesh['ind'=64,'snp'=4] {'snp'}, use_global_device_ids=true, to_apply=%region_0.0 | all-reduce | flops 22528 | bytes 90112 | tf_op jit(solution)/shard_map/psum | solution.py:38
  153.1 12.5 %convolution_bitcast_fusion = f32[32768,128]{0,1:T(8,128)} fusion(bf16[176,32768]{1,0:T(8,128)(2,1)} %param.7, bf16[176,128]{1,0:T(8,128)(2,1)S(1)} %psum.21, f32[176]{0:T(256)S(1)} %convert_element_type.24), kind=kOutput, calls=%fused_computation.3 | convolution fusion | flops 1476552704 | bytes 28357312 | tf_op jit(solution)/shard_map/dot_general | solution.py:45
  165.6 0.9 copy-done.2
  166.7 122.0 %all-reduce.3.cloned.1.call-done = f32[256,256]{0,1:T(8,128)} async-done(((f32[256,256]{0,1:T(8,128)}), f32[256,256]{0,1:T(8,128)}) %all-reduce.3.cloned.1.call-update) | async-done | bytes 262160 | tf_op jit(solution)/shard_map/psum | solution.py:55
  288.7 1.0 convert_add_fusion
  289.8 1.0 fusion.12
  290.8 11.7 %cholesky.50 = f32[128,128]{1,0:T(8,128)S(1)} custom-call(f32[128,128]{1,0:T(8,128)S(1)} %cholesky.118), custom_call_target="Cholesky" | custom-call | tf_op jit(solution)/shard_map/jit(cholesky)/cholesky | solution.py:14
  302.6 9.8 %custom-call.14 = f32[1,128,128]{1,2,0:T(8,128)S(1)} custom-call(f32[1,128,128]{2,1,0:T(8,128)S(1)} %get-tuple-element.30), custom_call_target="InvertDiagBlocksLowerTriangular" | custom-call | tf_op jit(solution)/shard_map/jit(cholesky)/cholesky | solution.py:14
  312.9 11.9 %cholesky.105 = f32[128,128]{1,0:T(8,128)S(1)} custom-call(f32[128,128]{1,0:T(8,128)S(1)} %convolution_subtract_fusion.1), custom_call_target="Cholesky" | custom-call | tf_op jit(solution)/shard_map/jit(cholesky)/cholesky | solution.py:14
  324.8 0.6 compare_reduce_fusion.1
  325.5 0.6 compare_reduce_fusion
  327.5 4.0 while.1
  327.5 0.6 fusion.57
  328.1 1.4 bitcast_dynamic-update-slice_fusion.2
  330.1 1.4 bitcast_dynamic-update-slice_fusion.2
  331.5 19.7 %custom-call.15 = f32[2,128,128]{1,2,0:T(8,128)S(1)} custom-call(f32[2,128,128]{2,1,0:T(8,128)S(1)} %get-tuple-element.12), custom_call_target="InvertDiagBlocksLowerTriangular" | custom-call | tf_op jit(solution)/shard_map/triangular_solve | solution.py:16
  351.2 2.3 gather_fusion
  353.6 0.6 log_reduce_fusion
  355.1 0.6 fusion.8
  355.8 0.7 multiply_reduce_fusion
  356.4 0.7 fusion.25
  357.8 208.4 %psum.23 = f32[]{:T(128)} all-reduce(f32[]{:T(128)} %fusion.25), channel_id=1, replica_groups=mesh['ind'=64,'snp'=4] {'ind'}, use_global_device_ids=true, to_apply=%region_11.12 | all-reduce | flops 1 | bytes 8 | tf_op jit(solution)/shard_map/psum | solution.py:40
  566.9 37.5 %reduce-scatter.2.cloned.1.call-done = f32[512,128]{0,1:T(8,128)} async-done(((f32[32768,128]{0,1:T(8,128)}), f32[512,128]{0,1:T(8,128)}) %reduce-scatter.2.cloned.1.call-update) | async-done | bytes 262160 | tf_op jit(solution)/shard_map/reduce_scatter | solution.py:44
  604.4 1.0 multiply_reduce_fusion.1
  605.4 0.6 divide_subtract_fusion
  606.0 2.4 fusion.1
  (36 shorter events, 2.9 us)
Async XLA Ops:
  8.0 0.9 copy-start
  8.0 119.6 %all-gather.2.cloned.1.call-start = ((), (), s32[]{:S(2)}) async-start(), calls=%async_computation.1 | async-start | bytes 8519680 | tf_op jit(solution)/shard_map/all_gather | solution.py:34
  11.3 277.4 %all-reduce.3.cloned.1.call-start = ((), (), s32[]{:S(2)}) async-start(), calls=%async_computation.3 | async-start | bytes 524288 | tf_op jit(solution)/shard_map/psum | solution.py:55
  14.4 589.9 %reduce-scatter.2.cloned.1.call-start = ((), (), s32[]{:S(2)}) async-start(), calls=%async_computation.2 | async-start | bytes 17039360 | tf_op jit(solution)/shard_map/reduce_scatter | solution.py:44
  165.6 0.9 copy-start.2
  165.6 190.2 %copy-start.1 = (f32[512,256]{1,0:T(8,128)S(1)}, f32[512,256]{1,0:T(8,128)}, u32[]{:S(2)}) copy-start(f32[512,256]{1,0:T(8,128)} %param.10) | copy-start | bytes 1572868
  165.6 439.8 %copy-start.3 = (f32[512]{0:T(512)S(1)}, f32[512]{0:T(512)}, u32[]{:S(2)}) copy-start(f32[512]{0:T(512)} %param.9) | copy-start | bytes 6148
  165.6 439.8 %copy-start.4 = (f32[512]{0:T(512)S(1)}, f32[512]{0:T(512)}, u32[]{:S(2)}) copy-start(f32[512]{0:T(512)} %param.11) | copy-start | bytes 6148
Sparse Core Ops, SparseCore 0:
  12.5 115.0 all-gather.1
  165.7 438.5 reduce-scatter.1
Sparse Core Ops, SparseCore 1:
  17.8 270.9 all-reduce.2
where the time goes:
time: 619 us; the launch traced here: 618 us
  waiting for transfers between devices  272 us (44%)
  blocking collectives  224 us (36%)
  other arithmetic  60.1 us (10%)
  matrix products  32.9 us (5%)
  between operations  20.6 us (3%)
  local copies, waits for them, and re-layouts  8.42 us (1%)
    psum x1, blocking collectives, on_device(): loglik_total = lax.psum(loglik_terms, 'ind')  208 us
    psum x1, waiting for transfers between devices, on_device(): gram_matrix = identity + lax.psum(gram_part, ('ind', 'snp'))  122 us
    all_gather x1, waiting for transfers between devices, on_device(): lax.all_gather(samples, 'ind', axis=0, tiled=True)  112 us
    reduce_scatter x1, waiting for transfers between devices, on_device(): lax.psum_scatter(lax.dot_general(columns, weights, (((0,), (0,)), ((), ()...  37.5 us
    another operation x7, other arithmetic, invert_gram(): factor_chol = jnp.linalg.cholesky(gram_matrix)  34.8 us
    another operation x3, other arithmetic, invert_gram(): lax.linalg.triangular_solve(factor_chol, identity, left_side=True, lower=...  19.7 us
    psum x1, blocking collectives, on_device(): lax.psum(partial_logits.astype(jnp.bfloat16), 'snp').astype(jnp.float32)  15.6 us
    dot_general x1, matrix products, on_device(): lax.dot_general(columns, weights, (((0,), (0,)), ((), ())), preferred_ele...  12.5 us
  transfers between devices with their start and end apart: 3, of which 3 were waited for; matrix products, arithmetic and copies ran while one was open for 15% of the time, Pallas kernels for 0%

commit v1 on v0

--- a/solution.py
+++ b/solution.py
@@ -19,6 +19,13 @@
 
 
 def on_device(dosages, phenotype, mean_effect, factor, log_scale, diag_noise, base_points):
+
+    def close_series_all(block_in, d_out):
+        return jnp.concatenate(
+            lax.all_to_all(jnp.stack(lax.axis_size("ind") * [block_in], axis=0), "ind", 0, 0),
+            axis=d_out,
+        )
+
     sample_count = base_points.shape[0]
     local_ind = dosages.shape[0]
     total_ind = local_ind * lax.axis_size("ind")
@@ -30,9 +37,7 @@
     )
     columns = dosages
     partial_logits = jnp.dot(
-        columns,
-        lax.all_gather(samples, "ind", axis=0, tiled=True),
-        preferred_element_type=jnp.float32,
+        columns, close_series_all(samples, 0), preferred_element_type=jnp.float32
     )
     labels = phenotype.astype(jnp.float32)[:, None]
     logits = lax.psum(partial_logits.astype(jnp.bfloat16), "snp").astype(jnp.float32)

time: 619 us -> 741 us (1.20)
  waiting for transfers between devices: 272 us -> 364 us
  blocking collectives: 224 us -> 238 us
  starting transfers between devices: 0.12 us -> 14.1 us
    all_to_all x0 -> x1, waiting for transfers between devices: none -> 184 us  [close_series_all(): lax.all_to_all(jnp.stack(lax.axis_size('ind') * [block_in], axis=0), 'ind...]
    all_gather x1 -> x0, waiting for transfers between devices: 112 us -> none  [on_device(): lax.all_gather(samples, 'ind', axis=0, tiled=True)]
    psum x1, waiting for transfers between devices: 122 us -> 180 us  [on_device(): gram_matrix = identity + lax.psum(gram_part, ('ind', 'snp'))]
    reduce_scatter x1, waiting for transfers between devices: 37.5 us -> 0.03 us  [on_device(): lax.psum_scatter(lax.dot_general(columns, weights, (((0,), (0,)), ((), ()...]
    all_to_all x0 -> x1, starting transfers between devices: none -> 14.1 us  [close_series_all(): lax.all_to_all(jnp.stack(lax.axis_size('ind') * [block_in], axis=0), 'ind...]
    psum x1, blocking collectives: 15.6 us -> 27.3 us  [on_device(): lax.psum(partial_logits.astype(jnp.bfloat16), 'snp').astype(jnp.float32)]
  transfers between devices with their start and end apart: 3 -> 3, of which waited for: 3 -> 2; matrix products, arithmetic and copies ran while one was open for 15% -> 12% of each run, Pallas kernels for 0% -> 0%
where the time goes in v1:
time: 741 us
  waiting for transfers between devices  364 us (49%)
  blocking collectives  238 us (32%)
  other arithmetic  59.4 us (8%)
  matrix products  30.9 us (4%)
  between operations  20.6 us (3%)
  starting transfers between devices  14.1 us (2%)
  local copies, waits for them, and re-layouts  13.7 us (2%)
    psum x1, blocking collectives, on_device(): loglik_total = lax.psum(loglik_terms, 'ind')  211 us
    all_to_all x1, waiting for transfers between devices, close_series_all(): lax.all_to_all(jnp.stack(lax.axis_size('ind') * [block_in], axis=0), 'ind...  184 us
    psum x1, waiting for transfers between devices, on_device(): gram_matrix = identity + lax.psum(gram_part, ('ind', 'snp'))  180 us
    another operation x7, other arithmetic, invert_gram(): factor_chol = jnp.linalg.cholesky(gram_matrix)  34.8 us
    psum x1, blocking collectives, on_device(): lax.psum(partial_logits.astype(jnp.bfloat16), 'snp').astype(jnp.float32)  27.3 us
    another operation x3, other arithmetic, invert_gram(): lax.linalg.triangular_solve(factor_chol, identity, left_side=True, lower=...  19.7 us
  transfers between devices with their start and end apart: 3, of which 2 were waited for; matrix products, arithmetic and copies ran while one was open for 12% of the time, Pallas kernels for 0%

profile of v1, /device:TPU:32, one launch (start us, length us, event | category | flops | bytes accessed | tf_op | source)
XLA Modules:
  0.0 741.0 jit_solution(7549831057229343768)
XLA Ops:
  8.0 0.7 exp.10
  8.9 1.7 fusion.4
  10.6 5.2 stack.2
  15.9 14.1 %all-to-all-start = ((bf16[64,512,128]{2,1,0:T(8,128)(2,1)}), bf16[64,512,128]{2,1,0:T(8,128)(2,1)}, u32[]{:S(2)}, u32[]{:S(2)}) async-start(bf16[64,512,128]{2,1,0:T(8,128)(2,1)} %stack.2), calls=%async_computation | async-start | bytes 16777216 | tf_op jit(solution)/shard_map/all_to_all | solution.py:25
  30.0 1.9 fusion.6
  32.0 184.0 %all-to-all-done = bf16[64,512,128]{2,1,0:T(8,128)(2,1)} async-done(((bf16[64,512,128]{2,1,0:T(8,128)(2,1)}), bf16[64,512,128]{2,1,0:T(8,128)(2,1)}, u32[]{:S(2)}, u32[]{:S(2)}) %all-to-all-start) | async-done | bytes 8388640 | tf_op jit(solution)/shard_map/all_to_all | solution.py:25
  216.0 9.8 %fusion.5 = bf16[176,128]{1,0:T(8,128)(2,1)S(1)} fusion(bf16[176,32768]{1,0:T(8,128)(2,1)} %param.7, bf16[32768,128]{1,0:T(8,128)(2,1)} %bitcast), kind=kOutput, calls=%fused_computation.15 | convolution fusion | flops 1476417536 | bytes 19968000 | tf_op jit(solution)/shard_map/dot_general | solution.py:39
  225.9 27.3 %psum.21 = bf16[176,128]{1,0:T(8,128)(2,1)S(1)} all-reduce(bf16[176,128]{1,0:T(8,128)(2,1)S(1)} %fusion.5), channel_id=1, replica_groups=mesh['ind'=64,'snp'=4] {'snp'}, use_global_device_ids=true, to_apply=%region_0.0 | all-reduce | flops 22528 | bytes 90112 | tf_op jit(solution)/shard_map/psum | solution.py:43
  253.2 12.4 %convolution_bitcast_fusion = f32[32768,128]{0,1:T(8,128)} fusion(bf16[176,32768]{1,0:T(8,128)(2,1)} %param.7, bf16[176,128]{1,0:T(8,128)(2,1)S(1)} %psum.21, f32[176]{0:T(256)S(1)} %convert_element_type.24), kind=kOutput, calls=%fused_computation.3 | convolution fusion | flops 1476552704 | bytes 28357312 | tf_op jit(solution)/shard_map/dot_general | solution.py:50
  265.7 0.9 copy-done.2
  266.8 180.1 %all-reduce.3.cloned.1.call-done = f32[256,256]{0,1:T(8,128)} async-done(((f32[256,256]{0,1:T(8,128)}), f32[256,256]{0,1:T(8,128)}) %all-reduce.3.cloned.1.call-update) | async-done | bytes 262160 | tf_op jit(solution)/shard_map/psum | solution.py:60
  446.9 1.0 convert_add_fusion
  448.1 1.0 fusion.12
  449.1 11.7 %cholesky.50 = f32[128,128]{1,0:T(8,128)S(1)} custom-call(f32[128,128]{1,0:T(8,128)S(1)} %cholesky.118), custom_call_target="Cholesky" | custom-call | tf_op jit(solution)/shard_map/jit(cholesky)/cholesky | solution.py:14
  460.8 9.8 %custom-call.14 = f32[1,128,128]{1,2,0:T(8,128)S(1)} custom-call(f32[1,128,128]{2,1,0:T(8,128)S(1)} %get-tuple-element.30), custom_call_target="InvertDiagBlocksLowerTriangular" | custom-call | tf_op jit(solution)/shard_map/jit(cholesky)/cholesky | solution.py:14
  471.1 11.9 %cholesky.105 = f32[128,128]{1,0:T(8,128)S(1)} custom-call(f32[128,128]{1,0:T(8,128)S(1)} %convolution_subtract_fusion.1), custom_call_target="Cholesky" | custom-call | tf_op jit(solution)/shard_map/jit(cholesky)/cholesky | solution.py:14
  483.1 0.6 compare_reduce_fusion.1
  483.7 0.6 compare_reduce_fusion
  485.8 4.0 while.1
  485.8 0.6 fusion.57
  486.4 1.4 bitcast_dynamic-update-slice_fusion.2
  488.4 1.4 bitcast_dynamic-update-slice_fusion.2
  489.8 19.7 %custom-call.15 = f32[2,128,128]{1,2,0:T(8,128)S(1)} custom-call(f32[2,128,128]{2,1,0:T(8,128)S(1)} %get-tuple-element.12), custom_call_target="InvertDiagBlocksLowerTriangular" | custom-call | tf_op jit(solution)/shard_map/triangular_solve | solution.py:16
  509.5 2.3 gather_fusion
  511.8 0.6 log_reduce_fusion
  513.4 0.6 fusion.8
  514.0 0.7 multiply_reduce_fusion
  514.7 0.7 fusion.25
  516.0 210.5 %psum.23 = f32[]{:T(128)} all-reduce(f32[]{:T(128)} %fusion.25), channel_id=1, replica_groups=mesh['ind'=64,'snp'=4] {'ind'}, use_global_device_ids=true, to_apply=%region_11.12 | all-reduce | flops 1 | bytes 8 | tf_op jit(solution)/shard_map/psum | solution.py:45
  727.3 1.0 multiply_reduce_fusion.1
  728.3 0.6 divide_subtract_fusion
  728.9 2.4 fusion.1
  (38 shorter events, 2.9 us)
Async XLA Ops:
  8.0 0.9 copy-start
  10.6 19.4 %copy-start.1 = (f32[512,256]{1,0:T(8,128)S(1)}, f32[512,256]{1,0:T(8,128)}, u32[]{:S(2)}) copy-start(f32[512,256]{1,0:T(8,128)} %param.10) | copy-start | bytes 1572868
  15.9 16.1 %copy-start.5 = (s32[176]{0:T(256)S(1)}, s32[176]{0:T(256)}, u32[]{:S(2)}) copy-start(s32[176]{0:T(256)} %param.8) | copy-start | bytes 2116
  15.9 200.1 %all-to-all-start = ((bf16[64,512,128]{2,1,0:T(8,128)(2,1)}), bf16[64,512,128]{2,1,0:T(8,128)(2,1)}, u32[]{:S(2)}, u32[]{:S(2)}) async-start(bf16[64,512,128]{2,1,0:T(8,128)(2,1)} %stack.2), calls=%async_computation | async-start | bytes 16777216 | tf_op jit(solution)/shard_map/all_to_all | solution.py:25
  30.0 417.0 %all-reduce.3.cloned.1.call-start = ((), (), s32[]{:S(2)}) async-start(), calls=%async_computation.3 | async-start | bytes 524288 | tf_op jit(solution)/shard_map/psum | solution.py:60
  31.9 695.3 %reduce-scatter.2.cloned.1.call-start = ((), (), s32[]{:S(2)}) async-start(), calls=%async_computation.2 | async-start | bytes 17039360 | tf_op jit(solution)/shard_map/reduce_scatter | solution.py:49
  265.6 0.9 copy-start.2
  265.6 462.6 %copy-start.3 = (f32[512]{0:T(512)S(1)}, f32[512]{0:T(512)}, u32[]{:S(2)}) copy-start(f32[512]{0:T(512)} %param.9) | copy-start | bytes 6148
  265.6 462.6 %copy-start.4 = (f32[512]{0:T(512)S(1)}, f32[512]{0:T(512)}, u32[]{:S(2)}) copy-start(f32[512]{0:T(512)} %param.11) | copy-start | bytes 6148
Sparse Core Ops, SparseCore 0:
  36.8 410.0 all-reduce.2
Sparse Core Ops, SparseCore 1:
  265.8 443.0 reduce-scatter.1

commit v2 on v0

--- a/solution.py
+++ b/solution.py
@@ -3,11 +3,20 @@
 import jax.numpy as jnp
 from jax import lax
 from jax.sharding import PartitionSpec as P
+from jax.lax import psum
 
 P_SIZE = 131072
 R = 256
 S = 128
 COHORT_RATIO = 40
+
+
+def _part_region(arr):
+    across = "ind"
+    dev_axis = "snp"
+    for d in (dev_axis, across):
+        arr = psum(arr, axis_name=d)
+    return arr
 
 
 def invert_gram(gram_matrix):
@@ -52,7 +61,7 @@
     scaled = factor / spread[:, None]
     identity = jnp.eye(R, dtype=jnp.float32)
     gram_part = jnp.dot(scaled.T, scaled, precision=lax.Precision.HIGHEST)
-    gram_matrix = identity + lax.psum(gram_part, ("ind", "snp"))
+    gram_matrix = identity + _part_region(gram_part)
     factor_chol, inverse = invert_gram(gram_matrix)
     rank_entropy = jnp.sum(jnp.log(jnp.diagonal(factor_chol))) / R
     projected = jnp.dot(factor, inverse, precision=lax.Precision.HIGHEST)

time: 619 us -> 1320 us (2.13)
  waiting for transfers between devices: 272 us -> 972 us
    psum x1 -> x2, waiting for transfers between devices: 122 us -> 749 us  [_part_region(): arr = psum(arr, axis_name=d)]
    reduce_scatter x1, waiting for transfers between devices: 37.5 us -> 160 us  [on_device(): lax.psum_scatter(lax.dot_general(columns, weights, (((0,), (0,)), ((), ()...]
    all_gather x1, waiting for transfers between devices: 112 us -> 62.6 us  [on_device(): lax.all_gather(samples, 'ind', axis=0, tiled=True)]
  transfers between devices with their start and end apart: 3 -> 4, of which waited for: 3 -> 4; matrix products, arithmetic and copies ran while one was open for 15% -> 7% of each run, Pallas kernels for 0% -> 0%
where the time goes in v2:
time: 1320 us
  waiting for transfers between devices  972 us (74%)
  blocking collectives  228 us (17%)
  other arithmetic  60.1 us (5%)
  matrix products  32.8 us (2%)
  between operations  20.7 us (2%)
    psum x2, waiting for transfers between devices, _part_region(): arr = psum(arr, axis_name=d)  749 us
    psum x1, blocking collectives, on_device(): loglik_total = lax.psum(loglik_terms, 'ind')  212 us
    reduce_scatter x1, waiting for transfers between devices, on_device(): lax.psum_scatter(lax.dot_general(columns, weights, (((0,), (0,)), ((), ()...  160 us
    all_gather x1, waiting for transfers between devices, on_device(): lax.all_gather(samples, 'ind', axis=0, tiled=True)  62.6 us
    another operation x7, other arithmetic, invert_gram(): factor_chol = jnp.linalg.cholesky(gram_matrix)  34.8 us
  transfers between devices with their start and end apart: 4, of which 4 were waited for; matrix products, arithmetic and copies ran while one was open for 7% of the time, Pallas kernels for 0%

profile of v2, /device:TPU:32, one launch (start us, length us, event | category | flops | bytes accessed | tf_op | source)
XLA Modules:
  0.0 1321.9 jit_solution(16298854465886490964)
XLA Ops:
  8.1 0.7 exp.10
  8.8 3.1 fusion.6
  11.9 2.4 fusion.4
  14.4 0.7 convert_element_type.24
  15.1 53.9 %all-reduce.4.cloned.1.call-done = f32[256,256]{0,1:T(8,128)} async-done(((f32[256,256]{0,1:T(8,128)}), f32[256,256]{0,1:T(8,128)}) %all-reduce.4.cloned.1.call-update) | async-done | bytes 262160 | tf_op jit(solution)/shard_map/psum | solution.py:18
  69.0 62.6 %all-gather.2.cloned.1.call-done = bf16[32768,128]{1,0:T(8,128)(2,1)} async-done(((bf16[512,128]{1,0:T(8,128)(2,1)}), bf16[32768,128]{1,0:T(8,128)(2,1)}) %all-gather.2.cloned.1.call-update) | async-done | bytes 8388624 | tf_op jit(solution)/shard_map/all_gather | solution.py:43
  131.7 9.8 fusion.5
  141.5 15.6 %psum.28 = bf16[176,128]{1,0:T(8,128)(2,1)S(1)} all-reduce(bf16[176,128]{1,0:T(8,128)(2,1)S(1)} %fusion.5), channel_id=1, replica_groups=mesh['ind'=64,'snp'=4] {'snp'}, use_global_device_ids=true, to_apply=%region_0.0 | all-reduce | flops 22528 | bytes 90112 | tf_op jit(solution)/shard_map/psum | solution.py:47
  157.1 12.4 convolution_bitcast_fusion
  169.6 0.9 copy-done.2
  170.7 694.9 %all-reduce.6.cloned.1.call-done = f32[256,256]{0,1:T(8,128)} async-done(((f32[256,256]{0,1:T(8,128)}), f32[256,256]{0,1:T(8,128)}) %all-reduce.6.cloned.1.call-update) | async-done | bytes 262160 | tf_op jit(solution)/shard_map/psum | solution.py:18
  865.6 1.0 convert_add_fusion
  866.7 1.0 fusion.12
  867.8 11.7 cholesky.50
  879.5 9.8 custom-call.14
  889.8 11.9 cholesky.105
  901.7 0.6 compare_reduce_fusion.1
  902.4 0.6 compare_reduce_fusion
  904.5 4.0 while.1
  905.1 1.4 bitcast_dynamic-update-slice_fusion.2
  907.1 1.4 bitcast_dynamic-update-slice_fusion.2
  908.5 19.7 %custom-call.15 = f32[2,128,128]{1,2,0:T(8,128)S(1)} custom-call(f32[2,128,128]{2,1,0:T(8,128)S(1)} %get-tuple-element.12), custom_call_target="InvertDiagBlocksLowerTriangular" | custom-call | tf_op jit(solution)/shard_map/triangular_solve | solution.py:25
  928.1 2.3 gather_fusion
  930.5 0.6 log_reduce_fusion
  932.1 0.6 fusion.8
  932.7 0.7 multiply_reduce_fusion
  933.4 0.7 fusion.25
  934.7 212.2 %psum.31 = f32[]{:T(128)} all-reduce(f32[]{:T(128)} %fusion.25), channel_id=1, replica_groups=mesh['ind'=64,'snp'=4] {'ind'}, use_global_device_ids=true, to_apply=%region_12.13 | all-reduce | flops 1 | bytes 8 | tf_op jit(solution)/shard_map/psum | solution.py:49
  1147.5 160.5 %reduce-scatter.2.cloned.1.call-done = f32[512,128]{0,1:T(8,128)} async-done(((f32[32768,128]{0,1:T(8,128)}), f32[512,128]{0,1:T(8,128)}) %reduce-scatter.2.cloned.1.call-update) | async-done | bytes 262160 | tf_op jit(solution)/shard_map/reduce_scatter | solution.py:53
  1308.0 1.0 multiply_reduce_fusion.1
  1309.0 0.6 divide_subtract_fusion
  1309.6 2.4 fusion.1
  (39 shorter events, 3.4 us)
Async XLA Ops:
  8.0 3.9 copy-start
  8.0 60.9 %all-reduce.4.cloned.1.call-start = ((), (), s32[]{:S(2)}) async-start(), calls=%async_computation.3 | async-start | bytes 524288 | tf_op jit(solution)/shard_map/psum | solution.py:18
  11.9 119.8 %all-gather.2.cloned.1.call-start = ((), (), s32[]{:S(2)}) async-start(), calls=%async_computation.1 | async-start | bytes 8519680 | tf_op jit(solution)/shard_map/all_gather | solution.py:43
  14.3 851.3 %all-reduce.6.cloned.1.call-start = ((), (), s32[]{:S(2)}) async-start(), calls=%async_computation.4 | async-start | bytes 524288 | tf_op jit(solution)/shard_map/psum | solution.py:18
  69.0 1239.1 %reduce-scatter.2.cloned.1.call-start = ((), (), s32[]{:S(2)}) async-start(), calls=%async_computation.2 | async-start | bytes 17039360 | tf_op jit(solution)/shard_map/reduce_scatter | solution.py:53
  169.6 0.9 copy-start.2
  169.6 763.1 %copy-start.1 = (f32[512,256]{1,0:T(8,128)S(1)}, f32[512,256]{1,0:T(8,128)}, u32[]{:S(2)}) copy-start(f32[512,256]{1,0:T(8,128)} %param.10) | copy-start | bytes 1572868
  169.6 1139.5 %copy-start.3 = (f32[512]{0:T(512)S(1)}, f32[512]{0:T(512)}, u32[]{:S(2)}) copy-start(f32[512]{0:T(512)} %param.9) | copy-start | bytes 6148
  169.6 1139.5 %copy-start.4 = (f32[512]{0:T(512)S(1)}, f32[512]{0:T(512)}, u32[]{:S(2)}) copy-start(f32[512]{0:T(512)} %param.11) | copy-start | bytes 6148
Sparse Core Ops, SparseCore 0:
  12.1 56.8 all-reduce.3
Sparse Core Ops, SparseCore 1:
  16.0 115.6 all-gather.1
  134.3 731.2 all-reduce.5
  868.1 439.9 reduce-scatter.1
